TPU v7x, 256 devices: a whole 4x4x8 slice. The times are simulated.
256 devices in a mesh: pair: 16 (over z_hi, y, core), aux: 16 (over x, z_lo).
Axes of the slice: x: 4, y: 4, z: 8 (z_hi: 2, z_lo: 4; z = z_hi * 4 + z_lo), core: 2. Of those that a mesh axis runs over, the one named last changes fastest.
Arguments:
- three_index: float32 [32, 768, 8192], P('pair', None, 'aux'), may hold values from -0.6 to 0.6
- occupied_energy: float32 [32], P('pair'), may hold values from -2 to -0.5
- virtual_energy: float32 [768], replicated, may hold values from 0.2 to 3
- plan: int32 [2, 32], P(None, 'pair'), may hold values from 0 to 1, as said below
Outputs:
- gradient_blocks: float32 [32, 768, 8192], P('pair', None, 'aux')
- virtual_density: float32 [768, 768], P('aux', 'pair')
Inputs may be any that keep to these rules, and one draw needn't show every extreme that they name: For block p and round r with q = p XOR 2**r: the row plan[r, p * 2 : (p + 1) * 2] is a permutation of the slots, and plan[r, q * 2 + plan[r, p * 2 + k]] = k, so every orbital is paired with exactly one orbital of block q in each round.
All inputs are finite; a program needn't handle non-finite values.
Results may differ from a plain program's by a relative error of at most 0.0001.
Values sent between devices are 32-bit elements; how exact they have to be, the bound alone decides.
A program may use at most 128 MiB of HBM per device.

v0:
```python
import jax
import jax.numpy as jnp
from jax import lax
from jax.sharding import PartitionSpec as P


def swapped(block, axis, bit):
    count = lax.axis_size(axis)
    route = []
    for low in range(count):
        high = low | 1 << bit
        if high != low and high < count:
            route += [(low, high), (high, low)]
    return lax.ppermute(block, axis, route)


def body(three_index, occupied_energy, virtual_energy, plan):
    highest = lax.Precision.HIGHEST
    per_block = three_index.shape[0]
    half_count = per_block // 2
    width = three_index.shape[1]
    row_count = width // lax.axis_size("aux")
    row_start = lax.axis_index("aux") * row_count
    position = lax.axis_index("pair")
    slots = jnp.arange(per_block, dtype=jnp.int32)
    lower_slots = slots[:half_count]
    upper_slots = slots[half_count:]
    gradient = jnp.zeros(three_index.shape, jnp.float32)
    density = jnp.zeros((row_count, width), jnp.float32)
    for turn_index in range(plan.shape[0]):
        table = plan[turn_index]
        upper_side = position // 2**turn_index % 2 == 1
        inverse = jnp.sum(jnp.where(table[None, :] == slots[:, None], slots[None, :], 0), axis=1)
        own_slots = jnp.where(upper_side, inverse[half_count:], lower_slots)
        peer_slots = jnp.where(upper_side, upper_slots, table[:half_count])
        send_slots = jnp.where(upper_side, inverse[:half_count], upper_slots)
        own_blocks = jnp.take(three_index, own_slots, axis=0)
        own_energy = jnp.take(occupied_energy, own_slots)
        peer_all, energy_all = swapped((three_index, occupied_energy), "pair", turn_index)
        peer_blocks = jnp.take(peer_all, peer_slots, axis=0)
        peer_energy = jnp.take(energy_all, peer_slots)
        pair_energy = own_energy + peer_energy
        partial_value = jnp.einsum(
            "hap,hbp->ahb",
            own_blocks,
            peer_blocks,
            precision=highest,
            preferred_element_type=jnp.float32,
        )
        summed = lax.psum(partial_value, "aux")
        gap_full = (
            pair_energy[None, :, None]
            - virtual_energy[:, None, None]
            - virtual_energy[None, None, :]
        )
        amplitude = summed / gap_full
        tilde = 2.0 * amplitude - jnp.transpose(amplitude, (2, 1, 0))
        amp_rows = lax.dynamic_slice_in_dim(amplitude, row_start, row_count, 0)
        amp_columns = lax.dynamic_slice_in_dim(amplitude, row_start, row_count, 2)
        density = density + jnp.einsum(
            "ahc,bhc->ab", amp_rows, tilde, precision=highest, preferred_element_type=jnp.float32
        )
        density = density + jnp.einsum(
            "cha,chb->ab", amp_columns, tilde, precision=highest, preferred_element_type=jnp.float32
        )
        own_term = jnp.einsum(
            "ahb,hbp->hap",
            tilde,
            peer_blocks,
            precision=highest,
            preferred_element_type=jnp.float32,
        )
        peer_term = jnp.einsum(
            "ahb,hap->hbp", tilde, own_blocks, precision=highest, preferred_element_type=jnp.float32
        )
        returned = swapped(peer_term, "pair", turn_index)
        gradient = gradient.at[own_slots].add(own_term)
        gradient = gradient.at[send_slots].add(returned)
    density = lax.psum_scatter(density, "pair", scatter_dimension=1, tiled=True)
    return (gradient, density)


def solution(mesh):
    in_specs = (P("pair", None, "aux"), P("pair"), P(), P(None, "pair"))
    out_specs = (P("pair", None, "aux"), P("aux", "pair"))
    return jax.shard_map(body, mesh=mesh, in_specs=in_specs, out_specs=out_specs, check_vma=False)
```

profile of v0, /device:TPU:2, one launch (start us, length us, event | category | flops | bytes accessed | tf_op | source)
XLA Modules:
  0.0 451.5 jit_solution(10524392798623498606)
XLA Ops:
  7.2 0.0 all-reduce.3.cloned.1.call-start
  7.2 0.1 collective-permute-start
  7.3 1.7 collective-permute-start.3
  9.0 0.8 slice_bitcast_fusion
  9.7 0.1 fusion.86
  9.9 0.6 fusion.97
  11.1 0.6 slice.125
  11.8 1.3 fusion.94
  15.7 0.6 fusion.95
  17.0 0.0 collective-permute-done
  17.0 0.0 copy-start.6
  17.0 0.0 copy-start.3
  17.0 7.9 %convolution_bitcast_fusion.1 = f32[768,1,768]{0,2,1:T(8,128)} fusion(f32[2,768,512]{2,1,0:T(8,128)S(1)} %collective-permute-done, s32[]{:T(128)} %bitcast.4, f32[2,768,512]{2,1,0:T(8,128)} %param.14, s32[]{:T(128)} %bitcast.7, pred[]{:T(512)} %bitcast.6, pred[]{:T(512)} %bitcast.3), kind=kOutput, calls=%fused_computation.24 | convolution fusion | flops 3624665088 | bytes 5507072 | tf_op jit(solution)/shard_map/hap,hbp->ahb/dot_general | solution.py:43
  25.0 0.0 copy-done.6
  25.0 53.2 %collective-permute-done.3 = f32[2,768,512]{2,1,0:T(8,128)} collective-permute-done((f32[2,768,512]{2,1,0:T(8,128)}, f32[2,768,512]{2,1,0:T(8,128)}, u32[]{:S(2)}, u32[]{:S(2)}) %collective-permute-start.3) | collective-permute-done | bytes 3145760 | tf_op jit(solution)/shard_map/ppermute | solution.py:14
  78.1 0.0 copy-done.3
  78.1 6.9 %convolution_bitcast_fusion = f32[768,1,768]{0,2,1:T(8,128)} fusion(f32[2,768,512]{2,1,0:T(8,128)} %collective-permute-done.3, s32[]{:T(128)} %bitcast.24, f32[2,768,512]{2,1,0:T(8,128)S(1)} %copy-done.3, s32[]{:T(128)} %bitcast.21, pred[]{:T(512)} %bitcast.26, pred[]{:T(512)} %bitcast.23), kind=kOutput, calls=%fused_computation.23 | convolution fusion | flops 3624665088 | bytes 5507072 | tf_op jit(solution)/shard_map/hap,hbp->ahb/dot_general | solution.py:43
  85.0 0.0 copy-start.9
  85.0 0.0 copy-start.10
  85.0 0.0 all-reduce.3.cloned.1.call-update
  85.0 0.0 reduce-scatter.4.cloned.1.call-start
  85.1 0.6 copy-done.9
  85.7 1.6 collective-permute-start.4
  87.2 0.4 collective-permute-start.1
  90.1 0.6 fusion.96
  91.9 0.0 copy-done.10
  91.9 0.8 and_reduce_fusion
  92.7 0.0 collective-permute-done.4
  92.7 0.6 dynamic-slice.53
  93.9 0.0 collective-permute-done.1
  93.9 0.6 dynamic-slice.51
  95.2 0.0 copy-done.8
  95.2 213.8 %all-reduce.3.cloned.1.call-done = (f32[768,1,768]{0,2,1:T(8,128)}, f32[768,1,768]{0,2,1:T(8,128)}) async-done(((f32[768,1,768]{0,2,1:T(8,128)}, f32[768,1,768]{0,2,1:T(8,128)}), (f32[768,1,768]{0,2,1:T(8,128)}, f32[768,1,768]{0,2,1:T(8,128)})) %all-reduce.3.cloned.1.call-update) | async-done | bytes 4718608 | tf_op jit(solution)/shard_map/psum | solution.py:50
  309.0 4.5 subtract_divide_fusion
  313.5 1.5 copy-done.2
  315.0 2.0 copy.10
  317.0 2.8 bitcast_subtract_fusion.1
  319.9 0.5 copy-done.4
  320.3 5.0 %fusion.27 = f32[1,768,512]{2,1,0:T(8,128)} fusion(f32[768,1,768]{2,0,1:T(8,128)S(1)} %bitcast_subtract_fusion.1, f32[2,768,512]{2,1,0:T(8,128)S(1)} %copy-done.4, s32[]{:T(128)} %bitcast.7, pred[]{:T(512)} %bitcast.6), kind=kOutput, calls=%fused_computation.41 | convolution fusion | flops 3624271872 | bytes 5505029 | tf_op jit(solution)/shard_map/ahb,hap->hbp/dot_general | solution.py:73
  325.4 0.0 collective-permute-start.2
  325.4 3.1 copy.11
  328.5 2.8 bitcast_subtract_fusion
  331.3 0.5 copy-done.5
  331.8 5.1 %fusion.32 = f32[1,768,512]{2,1,0:T(8,128)} fusion(f32[768,1,768]{2,0,1:T(8,128)S(1)} %bitcast_subtract_fusion, f32[2,768,512]{2,1,0:T(8,128)S(1)} %copy-done.5, s32[]{:T(128)} %bitcast.21, pred[]{:T(512)} %bitcast.26), kind=kOutput, calls=%fused_computation.42 | convolution fusion | flops 3624271872 | bytes 5505029 | tf_op jit(solution)/shard_map/ahb,hap->hbp/dot_general | solution.py:73
  336.9 1.6 collective-permute-start.5
  338.5 3.4 fusion.2
  341.9 2.4 fusion.8
  344.3 3.3 fusion.48
  347.7 0.0 copy-done
  347.7 2.4 fusion.51
  350.1 1.0 copy.12
  351.1 0.0 reduce-scatter.4.cloned.1.call-update
  351.1 0.0 copy-start.7
  351.1 2.1 broadcast_in_dim.57
  353.2 1.0 copy-done.7
  354.2 5.6 %bitcast_dynamic-update-slice_fusion = f32[2,768,512]{2,1,0:T(8,128)} fusion(f32[2,768,512]{2,1,0:T(8,128)} %broadcast_in_dim.57, s32[]{:T(128)} %bitcast.7, f32[768,1,768]{2,0,1:T(8,128)S(1)} %bitcast_subtract_fusion.1, f32[2,768,512]{2,1,0:T(8,128)S(1)} %copy-done.7, s32[]{:T(128)} %bitcast.4, pred[]{:T(512)} %bitcast.3, pred[]{:T(512)} %get-tuple-element.120), kind=kOutput, calls=%fused_computation.32 | convolution fusion | flops 3624665088 | bytes 5507072 | tf_op jit(solution)/shard_map/ahb,hbp->hap/dot_general | solution.py:66
  359.7 67.2 %reduce-scatter.4.cloned.1.call-done = f32[48,48]{1,0:T(8,128)} async-done(((f32[768,48]{1,0:T(8,128)}), f32[48,48]{1,0:T(8,128)}) %reduce-scatter.4.cloned.1.call-update) | async-done | bytes 9232
  427.0 1.4 copy.13
  428.4 0.0 collective-permute-done.2
  428.4 4.2 fusion.16
  432.6 0.0 copy-done.1
  432.6 7.8 %fusion.17 = f32[2,768,512]{2,1,0:T(8,128)} fusion(f32[2,768,512]{2,1,0:T(8,128)} %fusion.16, s32[]{:T(128)} %bitcast.21, f32[2,768,512]{2,1,0:T(8,128)} %collective-permute-done.3, s32[]{:T(128)} %bitcast.24, f32[768,1,768]{2,0,1:T(8,128)S(1)} %copy-done.1, pred[]{:T(512)} %bitcast.23, pred[]{:T(512)} %get-tuple-element.107), kind=kOutput, calls=%fused_computation.26 | convolution fusion | flops 3625058304 | bytes 7079936 | tf_op jit(solution)/shard_map/ahb,hbp->hap/dot_general | solution.py:66
  440.4 0.0 collective-permute-done.5
  440.4 4.0 fusion.18
  (9 shorter events, 0.0 us)
Async XLA Ops:
  7.2 301.8 %all-reduce.3.cloned.1.call-start = ((), (), s32[]{:S(2)}) async-start(), calls=%async_computation.2 | async-start | bytes 9437184 | tf_op jit(solution)/shard_map/psum | solution.py:50
  7.2 9.8 %collective-permute-start = (f32[2,768,512]{2,1,0:T(8,128)}, f32[2,768,512]{2,1,0:T(8,128)S(1)}, u32[]{:S(2)}, u32[]{:S(2)}) collective-permute-start(f32[2,768,512]{2,1,0:T(8,128)} %param.14), channel_id=1, source_target_pairs={{0,16},{16,0},{32,48},{48,32},{64,80},{80,64},{96,112},{112,96},{1... | collective-permute-start | bytes 9437192 | tf_op jit(solution)/shard_map/ppermute | solution.py:14
  7.3 70.8 %collective-permute-start.3 = (f32[2,768,512]{2,1,0:T(8,128)}, f32[2,768,512]{2,1,0:T(8,128)}, u32[]{:S(2)}, u32[]{:S(2)}) collective-permute-start(f32[2,768,512]{2,1,0:T(8,128)} %param.14), channel_id=1, source_target_pairs={{0,32},{32,0},{16,48},{48,16},{64,96},{96,64},{80,112},{112,80},{1... | collective-permute-start | bytes 9437192 | tf_op jit(solution)/shard_map/ppermute | solution.py:14
  17.0 8.0 %copy-start.6 = (f32[2,768,512]{2,1,0:T(8,128)}, f32[2,768,512]{2,1,0:T(8,128)S(1)}, u32[]{:S(2)}) copy-start(f32[2,768,512]{2,1,0:T(8,128)S(1)} %collective-permute-done) | copy-start | bytes 9437188
  17.0 61.1 %copy-start.3 = (f32[2,768,512]{2,1,0:T(8,128)S(1)}, f32[2,768,512]{2,1,0:T(8,128)}, u32[]{:S(2)}) copy-start(f32[2,768,512]{2,1,0:T(8,128)} %param.14) | copy-start | bytes 9437188
  85.0 0.7 copy-start.9
  85.0 6.9 %copy-start.10 = (s32[3]{0:T(128)S(1)}, s32[3]{0:T(128)}, u32[]{:S(2)}) copy-start(s32[3]{0:T(128)} %constant.173.clone.1) | copy-start | bytes 40
  85.0 10.2 %copy-start.8 = (f32[768]{0:T(1024)S(1)}, f32[768]{0:T(1024)}, u32[]{:S(2)}) copy-start(f32[768]{0:T(1024)} %param.16) | copy-start | bytes 9220
  85.0 342.0 %reduce-scatter.4.cloned.1.call-start = ((), (), s32[]{:S(2)}) async-start(), calls=%async_computation.1 | async-start | bytes 417792
  85.7 7.0 %collective-permute-start.4 = (f32[2]{0:T(128)S(1)}, f32[2]{0:T(128)S(1)}, u32[]{:S(2)}, u32[]{:S(2)}) collective-permute-start(f32[2]{0:T(128)S(1)} %copy-done.9), channel_id=1, source_target_pairs={{0,32},{32,0},{16,48},{48,16},{64,96},{96,64},{80,112},{112,80},{1... | collective-permute-start | bytes 32 | tf_op jit(solution)/shard_map/ppermute | solution.py:14
  87.2 6.7 %collective-permute-start.1 = (f32[2]{0:T(128)S(1)}, f32[2]{0:T(128)S(1)}, u32[]{:S(2)}, u32[]{:S(2)}) collective-permute-start(f32[2]{0:T(128)S(1)} %copy-done.9), channel_id=1, source_target_pairs={{0,16},{16,0},{32,48},{48,32},{64,80},{80,64},{96,112},{112,96},{1... | collective-permute-start | bytes 32 | tf_op jit(solution)/shard_map/ppermute | solution.py:14
  313.5 1.5 copy-start.2
  317.0 3.3 copy-start.4
  325.4 103.0 %collective-permute-start.2 = (f32[1,768,512]{2,1,0:T(8,128)}, f32[1,768,512]{2,1,0:T(8,128)}, u32[]{:S(2)}, u32[]{:S(2)}) collective-permute-start(f32[1,768,512]{2,1,0:T(8,128)} %fusion.27), channel_id=1, source_target_pairs={{0,16},{16,0},{32,48},{48,32},{64,80},{80,64},{96,112},{112,96},{1... | collective-permute-start | bytes 4718600 | tf_op jit(solution)/shard_map/ppermute | solution.py:14
  328.5 3.3 copy-start.5
  331.8 15.9 %copy-start = (f32[768,1,768]{2,0,1:T(8,128)}, f32[768,1,768]{2,0,1:T(8,128)S(1)}, u32[]{:S(2)}) copy-start(f32[768,1,768]{2,0,1:T(8,128)S(1)} %bitcast_subtract_fusion) | copy-start | bytes 7077892
  336.9 103.5 %collective-permute-start.5 = (f32[1,768,512]{2,1,0:T(8,128)}, f32[1,768,512]{2,1,0:T(8,128)}, u32[]{:S(2)}, u32[]{:S(2)}) collective-permute-start(f32[1,768,512]{2,1,0:T(8,128)} %fusion.32), channel_id=1, source_target_pairs={{0,32},{32,0},{16,48},{48,16},{64,96},{96,64},{80,112},{112,80},{1... | collective-permute-start | bytes 4718600 | tf_op jit(solution)/shard_map/ppermute | solution.py:14
  351.1 3.0 copy-start.7
  428.4 4.2 copy-start.1
Sparse Core Ops, SparseCore 0:
  85.1 223.8 all-reduce.2
  351.2 75.6 reduce-scatter.3
where the time goes:
time: 459 us; the launch traced here: 451 us
  waiting for transfers between devices  334 us (73%)
  matrix products  49.8 us (11%)
  between operations  23.3 us (5%)
  local copies, waits for them, and re-layouts  19.3 us (4%)
  other arithmetic  19.3 us (4%)
  starting transfers between devices  5.5 us (1%)
    psum x1, waiting for transfers between devices, body(): summed = lax.psum(partial_value, 'aux')  214 us
    unnamed x3, waiting for transfers between devices  67.3 us
    ppermute x6, waiting for transfers between devices, swapped(): return lax.ppermute(block, axis, route)  53.2 us
    dot_general x2, matrix products, body(): jnp.einsum('hap,hbp->ahb', own_blocks, peer_blocks, precision=highest, pr...  14.8 us
    dot_general x2, matrix products, body(): jnp.einsum('ahb,hbp->hap', tilde, peer_blocks, precision=highest, preferr...  13.4 us
    dot_general x2, matrix products, body(): jnp.einsum('ahb,hap->hbp', tilde, own_blocks, precision=highest, preferre...  10.1 us
  transfers between devices with their start and end apart: 8, of which 3 were waited for; matrix products, arithmetic and copies ran while one was open for 13% of the time, Pallas kernels for 0%

commit v1 on v0

--- a/solution.py
+++ b/solution.py
@@ -1,7 +1,16 @@
+import functools
 import jax
 import jax.numpy as jnp
 from jax import lax
 from jax.sharding import PartitionSpec as P
+from jax.lax import all_gather
+
+
+def _read_tables(field_in, across):
+    return jnp.sum(all_gather(field_in, across), 0)
+
+
+work_the_object = functools.partial(_read_tables, across="aux")
 
 
 def swapped(block, axis, bit):
@@ -47,7 +56,7 @@
             precision=highest,
             preferred_element_type=jnp.float32,
         )
-        summed = lax.psum(partial_value, "aux")
+        summed = work_the_object(partial_value)
         gap_full = (
             pair_energy[None, :, None]
             - virtual_energy[:, None, None]

time: 459 us -> 1830 us (3.99)
  waiting for transfers between devices: 334 us -> 1630 us
  local copies, waits for them, and re-layouts: 19.3 us -> 63.8 us
  other arithmetic: 19.3 us -> 51.5 us
    all_gather x0 -> x2, waiting for transfers between devices: none -> 1490 us  [_read_tables(): return jnp.sum(all_gather(field_in, across), 0)]
    psum x1 -> x0, waiting for transfers between devices: 214 us -> none  [body(): summed = lax.psum(partial_value, 'aux')]
    unnamed x24 -> x22, local copies, waits for them, and re-layouts: 6.39 us -> 50.9 us
    reduce_sum x0 -> x2, other arithmetic: none -> 32.4 us  [_read_tables(): return jnp.sum(all_gather(field_in, across), 0)]
    unnamed x3 -> x4, waiting for transfers between devices: 67.3 us -> 70.9 us
  transfers between devices with their start and end apart: 8 -> 9, of which waited for: 3 -> 5; matrix products, arithmetic and copies ran while one was open for 13% -> 5% of each run, Pallas kernels for 0% -> 0%
where the time goes in v1:
time: 1830 us; the launch traced here: 1820 us
  waiting for transfers between devices  1630 us (89%)
  local copies, waits for them, and re-layouts  63.8 us (3%)
  other arithmetic  51.5 us (3%)
  matrix products  50.7 us (3%)
  between operations  23.3 us (1%)
    all_gather x2, waiting for transfers between devices, _read_tables(): return jnp.sum(all_gather(field_in, across), 0)  1490 us
    unnamed x4, waiting for transfers between devices  70.9 us
    ppermute x6, waiting for transfers between devices, swapped(): return lax.ppermute(block, axis, route)  66.4 us
    unnamed x22, local copies, waits for them, and re-layouts  50.9 us
  transfers between devices with their start and end apart: 9, of which 5 were waited for; matrix products, arithmetic and copies ran while one was open for 5% of the time, Pallas kernels for 0%

profile of v1, /device:TPU:2, one launch (start us, length us, event | category | flops | bytes accessed | tf_op | source)
XLA Modules:
  0.0 1823.4 jit_solution(5636491314039703679)
XLA Ops:
  7.2 0.0 all-gather.7.cloned.1.call-start
  7.2 1.7 collective-permute-start.3
  8.9 0.6 slice.125
  9.5 1.3 fusion.94
  12.1 0.8 slice_bitcast_fusion
  12.9 0.1 fusion.86
  13.0 0.6 fusion.95
  14.3 63.0 %collective-permute-done.3 = f32[2,768,512]{2,1,0:T(8,128)S(1)} collective-permute-done((f32[2,768,512]{2,1,0:T(8,128)}, f32[2,768,512]{2,1,0:T(8,128)S(1)}, u32[]{:S(2)}, u32[]{:S(2)}) %collective-permute-start.3) | collective-permute-done | bytes 3145760 | tf_op jit(solution)/shard_map/ppermute | solution.py:23
  77.3 1.6 copy-done.5
  79.0 7.4 convolution_bitcast_fusion
  86.4 0.0 all-gather.7.cloned.1.call-update
  86.4 0.0 all-gather.5.cloned.1.call-start
  86.5 0.0 copy-done.3
  86.5 0.1 collective-permute-start
  86.6 0.6 fusion.97
  89.0 3.3 collective-permute-done
  92.4 6.8 convolution_bitcast_fusion.1
  99.1 0.0 all-gather.5.cloned.1.call-update
  99.2 0.0 reduce-scatter.4.cloned.1.call-start
  99.2 0.6 copy-done.7
  99.8 1.6 collective-permute-start.4
  101.4 0.5 collective-permute-start.1
  104.5 0.7 fusion.96
  106.5 0.0 copy-done.8
  106.5 0.8 and_reduce_fusion
  107.3 0.0 collective-permute-done.4
  107.3 0.6 dynamic-slice.53
  108.5 0.0 collective-permute-done.1
  108.5 0.6 dynamic-slice.51
  109.8 0.0 copy-done.6
  109.8 752.1 %all-gather.7.cloned.1.call-done = f32[12288,1,768]{0,2,1:T(8,128)} async-done(((f32[768,1,768]{0,2,1:T(8,128)}), f32[12288,1,768]{0,2,1:T(8,128)}) %all-gather.7.cloned.1.call-update) | async-done | bytes 37748752 | tf_op jit(solution)/shard_map/all_gather | solution.py:10
  861.9 22.4 %copy.15 = f32[96,8,16,768]{3,2,1,0:T(8,128)S(1)} copy(f32[96,8,16,768]{3,1,2,0:T(8,128)} %bitcast.135) | data formatting | bytes 75497472
  884.3 16.2 bitcast_reduce_fusion
  900.5 739.1 %all-gather.5.cloned.1.call-done = f32[12288,1,768]{0,2,1:T(8,128)} async-done(((f32[768,1,768]{0,2,1:T(8,128)}), f32[12288,1,768]{0,2,1:T(8,128)}) %all-gather.5.cloned.1.call-update) | async-done | bytes 37748752 | tf_op jit(solution)/shard_map/all_gather | solution.py:10
  1639.5 22.0 %copy.14 = f32[96,8,16,768]{3,2,1,0:T(8,128)S(1)} copy(f32[96,8,16,768]{3,1,2,0:T(8,128)} %bitcast.136) | data formatting | bytes 75497472
  1661.6 16.2 bitcast_reduce_fusion.1
  1677.8 4.5 bitcast_divide_fusion
  1682.3 1.4 copy-done.2
  1683.7 1.9 copy.10
  1685.6 2.7 bitcast_subtract_fusion.1
  1688.3 3.2 copy.11
  1691.5 0.0 copy-start.4
  1691.5 2.8 bitcast_subtract_fusion
  1694.3 0.5 copy-done.4
  1694.8 5.0 fusion.27
  1699.9 0.0 collective-permute-start.2
  1699.9 5.1 fusion.32
  1704.9 1.7 collective-permute-start.5
  1706.6 2.4 fusion.8
  1709.0 3.4 fusion.2
  1712.4 3.3 fusion.48
  1715.8 0.0 copy-done
  1715.8 2.4 fusion.51
  1718.2 0.9 copy.12
  1719.1 0.0 reduce-scatter.4.cloned.1.call-update
  1719.2 2.1 broadcast_in_dim.57
  1721.2 7.0 bitcast_dynamic-update-slice_fusion
  1728.2 70.9 %reduce-scatter.4.cloned.1.call-done = f32[48,48]{1,0:T(8,128)} async-done(((f32[768,48]{1,0:T(8,128)}), f32[48,48]{1,0:T(8,128)}) %reduce-scatter.4.cloned.1.call-update) | async-done | bytes 9232
  1799.1 1.4 copy.13
  1800.5 0.0 collective-permute-done.2
  1800.5 4.2 fusion.16
  1804.7 7.9 fusion.17
  1812.6 0.0 collective-permute-done.5
  1812.6 4.1 fusion.18
  (12 shorter events, 0.0 us)
Async XLA Ops:
  7.2 854.7 %all-gather.7.cloned.1.call-start = ((), (), s32[]{:S(2)}) async-start(), calls=%async_computation.2 | async-start | bytes 40108032 | tf_op jit(solution)/shard_map/all_gather | solution.py:10
  7.2 70.1 %collective-permute-start.3 = (f32[2,768,512]{2,1,0:T(8,128)}, f32[2,768,512]{2,1,0:T(8,128)S(1)}, u32[]{:S(2)}, u32[]{:S(2)}) collective-permute-start(f32[2,768,512]{2,1,0:T(8,128)} %param.14), channel_id=1, source_target_pairs={{0,32},{32,0},{16,48},{48,16},{64,96},{96,64},{80,112},{112,80},{1... | collective-permute-start | bytes 9437192 | tf_op jit(solution)/shard_map/ppermute | solution.py:23
  77.3 1.6 copy-start.5
  79.0 7.5 copy-start.3
  86.4 1553.1 %all-gather.5.cloned.1.call-start = ((), (), s32[]{:S(2)}) async-start(), calls=%async_computation.1 | async-start | bytes 40108032 | tf_op jit(solution)/shard_map/all_gather | solution.py:10
  86.5 5.9 collective-permute-start
  99.1 0.7 copy-start.7
  99.1 7.3 copy-start.8
  99.1 10.6 copy-start.6
  99.2 1699.9 %reduce-scatter.4.cloned.1.call-start = ((), (), s32[]{:S(2)}) async-start(), calls=%async_computation.3 | async-start | bytes 417792
  99.8 7.5 collective-permute-start.4
  101.4 7.1 collective-permute-start.1
  1682.3 1.4 copy-start.2
  1691.5 3.3 copy-start.4
  1694.8 21.0 %copy-start = (f32[768,1,768]{2,0,1:T(8,128)}, f32[768,1,768]{2,0,1:T(8,128)S(1)}, u32[]{:S(2)}) copy-start(f32[768,1,768]{2,0,1:T(8,128)S(1)} %bitcast_subtract_fusion) | copy-start | bytes 7077892
  1699.9 100.6 %collective-permute-start.2 = (f32[1,768,512]{2,1,0:T(8,128)}, f32[1,768,512]{2,1,0:T(8,128)}, u32[]{:S(2)}, u32[]{:S(2)}) collective-permute-start(f32[1,768,512]{2,1,0:T(8,128)} %fusion.27), channel_id=1, source_target_pairs={{0,16},{16,0},{32,48},{48,32},{64,80},{80,64},{96,112},{112,96},{1... | collective-permute-start | bytes 4718600 | tf_op jit(solution)/shard_map/ppermute | solution.py:23
  1704.9 107.6 %collective-permute-start.5 = (f32[1,768,512]{2,1,0:T(8,128)}, f32[1,768,512]{2,1,0:T(8,128)}, u32[]{:S(2)}, u32[]{:S(2)}) collective-permute-start(f32[1,768,512]{2,1,0:T(8,128)} %fusion.32), channel_id=1, source_target_pairs={{0,32},{32,0},{16,48},{48,16},{64,96},{96,64},{80,112},{112,80},{1... | collective-permute-start | bytes 4718600 | tf_op jit(solution)/shard_map/ppermute | solution.py:23
  1800.5 4.2 copy-start.1
Sparse Core Ops, SparseCore 0:
  86.5 775.2 all-gather.6
  863.7 775.8 all-gather.4
  1719.3 79.7 reduce-scatter.3
